TPU v7x, 32 devices: a whole 2x2x4 slice. The times are simulated.
32 devices in a mesh: ctx: 4 (over z), fsdp: 8 (over y, x, core).
Axes of the slice: x: 2, y: 2, z: 4, core: 2. Of those that a mesh axis runs over, the one named last changes fastest.
Arguments:
- tokens: bfloat16 [8, 512, 1024], P('fsdp', 'ctx'), may hold values from -12 to 12
- cotangent: bfloat16 [8, 512, 1024], P('fsdp', 'ctx'), may hold values from -6 to 6
- weight_rows: float32 [12288, 1024], P('fsdp'), may hold values from -2 to 2
- first_rows: float32 [12288, 1024], P('fsdp')
- second_rows: float32 [12288, 1024], P('fsdp'), as said below
- vector_rows: float32 [12, 1024], replicated, may hold values from -2 to 2
- vector_first: float32 [12, 1024], replicated
- vector_second: float32 [12, 1024], replicated, as said below
Outputs:
- output: bfloat16 [8, 512, 1024], P('fsdp', 'ctx')
- input_grad: float32 [8, 512, 1024], P('fsdp', 'ctx')
- weight_grad: float32 [12288, 1024], P('fsdp')
- new_weights: float32 [12288, 1024], P('fsdp')
- new_first: float32 [12288, 1024], P('fsdp')
- new_second: float32 [12288, 1024], P('fsdp')
- vector_grad: float32 [12, 1024], replicated
- new_vectors: float32 [12, 1024], replicated
- new_vector_first: float32 [12, 1024], replicated
- new_vector_second: float32 [12, 1024], replicated
Inputs may be any that keep to these rules, and one draw needn't show every extreme that they name: `second_rows`: every entry is positive. `vector_second`: every entry is positive.
All inputs are finite; a program needn't handle non-finite values.
Results may differ from a plain program's by a relative error of at most 0.025.
The roundings to bfloat16 on the way count: a program that leaves them out, or rounds other values in their place, can miss the bound.
Values may be sent and summed in bfloat16 or wider, within the bound.
No kernel may reach another device: no remote copies, remote signals or barrier semaphores. Data moves between devices by JAX's collectives and lax.ppermute only.
A program may use at most 320 MiB of HBM per device.

v0:
```python
import math
import jax
import jax.numpy as jnp
from jax import lax
from jax.sharding import PartitionSpec as P

D = 1024
HEADS = 16
beta_one = 0.9
beta_two = 0.999
learn_rate = 0.01
decay_rate = 0.01
adam_eps = 1e-08
norm_eps = 1e-05
adam_step = 2


def mat_nt(left, right):
    return lax.dot_general(
        left, right, (((1,), (1,)), ((), ())), preferred_element_type=jnp.float32
    )


def mat_tn(left, right):
    return lax.dot_general(
        left, right, (((0,), (0,)), ((), ())), preferred_element_type=jnp.float32
    )


def unpack(rows, vectors):
    width = rows.shape[1]
    hidden = (rows.shape[0] - 4 * width) // 2
    return [
        rows[: 3 * width],
        vectors[0],
        vectors[1],
        rows[3 * width : 4 * width],
        vectors[2],
        vectors[3],
        vectors[4],
        rows[4 * width : 4 * width + hidden],
        vectors[8:].reshape(hidden),
        rows[4 * width + hidden :],
        vectors[5],
        vectors[6],
        vectors[7],
    ]


def normalize(values):
    centred = values - jnp.mean(values, axis=-1, keepdims=True)
    inverse = lax.rsqrt(jnp.mean(centred * centred, axis=-1, keepdims=True) + norm_eps)
    return (centred * inverse, inverse)


def norm_back(grad_norm, normed, inverse):
    return inverse * (
        grad_norm
        - jnp.mean(grad_norm, axis=-1, keepdims=True)
        - normed * jnp.mean(grad_norm * normed, axis=-1, keepdims=True)
    )


def gelu_grad(pre_act):
    return (
        0.5 * (1.0 + lax.erf(pre_act * 0.7071067811865476))
        + pre_act * jnp.exp(-0.5 * pre_act * pre_act) * 0.3989422804014327
    )


def project(inputs, params):
    qkv_t, query_b, value_b = (params[0], params[1], params[2])
    width = qkv_t.shape[1]
    projected = mat_nt(inputs, qkv_t)
    query_rows = (projected[:, :width] + query_b.astype(jnp.float32)).astype(jnp.bfloat16)
    key_rows = projected[:, width : 2 * width].astype(jnp.bfloat16)
    value_rows = (projected[:, 2 * width :] + value_b.astype(jnp.float32)).astype(jnp.bfloat16)
    return (query_rows, key_rows, value_rows)


def tail_forward(inputs, attended, params):
    out_t, out_b, gain_one, shift_one, up_t, up_b, down_w, down_b, gain_two, shift_two = params[3:]
    first_sum = inputs.astype(jnp.float32) + mat_nt(attended, out_t) + out_b.astype(jnp.float32)
    normed_one, inverse_one = normalize(first_sum)
    hidden_in = normed_one * gain_one.astype(jnp.float32) + shift_one.astype(jnp.float32)
    hidden_b = hidden_in.astype(jnp.bfloat16)
    pre_act = mat_nt(hidden_b, up_t) + up_b.astype(jnp.float32)
    activ_b = jax.nn.gelu(pre_act, approximate=False).astype(jnp.bfloat16)
    second_sum = (
        hidden_in
        + jnp.dot(activ_b, down_w, preferred_element_type=jnp.float32)
        + down_b.astype(jnp.float32)
    )
    normed_two, inverse_two = normalize(second_sum)
    output = (normed_two * gain_two.astype(jnp.float32) + shift_two.astype(jnp.float32)).astype(
        jnp.bfloat16
    )
    return (output, (normed_one, inverse_one, hidden_b, pre_act, activ_b, normed_two, inverse_two))


def tail_backward(cotan, attended, saved, params):
    out_t, out_b, gain_one, shift_one, up_t, up_b, down_w, down_b, gain_two, shift_two = params[3:]
    normed_one, inverse_one, hidden_b, pre_act, activ_b, normed_two, inverse_two = saved
    grad_gain_two = jnp.sum(cotan * normed_two, axis=0)
    grad_shift_two = jnp.sum(cotan, axis=0)
    grad_second = norm_back(cotan * gain_two.astype(jnp.float32), normed_two, inverse_two)
    grad_second_b = grad_second.astype(jnp.bfloat16)
    grad_down_b = jnp.sum(grad_second, axis=0)
    grad_down_w = mat_tn(activ_b, grad_second_b)
    grad_pre = mat_nt(grad_second_b, down_w) * gelu_grad(pre_act)
    grad_pre_b = grad_pre.astype(jnp.bfloat16)
    grad_up_b = jnp.sum(grad_pre, axis=0)
    grad_up_t = mat_tn(grad_pre_b, hidden_b)
    grad_hidden = grad_second + jnp.dot(grad_pre_b, up_t, preferred_element_type=jnp.float32)
    grad_gain_one = jnp.sum(grad_hidden * normed_one, axis=0)
    grad_shift_one = jnp.sum(grad_hidden, axis=0)
    grad_first = norm_back(grad_hidden * gain_one.astype(jnp.float32), normed_one, inverse_one)
    grad_first_b = grad_first.astype(jnp.bfloat16)
    grad_out_b = jnp.sum(grad_first, axis=0)
    grad_out_t = mat_tn(grad_first_b, attended)
    grad_attended = jnp.dot(grad_first_b, out_t, preferred_element_type=jnp.float32).astype(
        jnp.bfloat16
    )
    tail_grads = (
        grad_out_t,
        grad_out_b,
        grad_gain_one,
        grad_shift_one,
        grad_up_t,
        grad_up_b,
        grad_down_w,
        grad_down_b,
        grad_gain_two,
        grad_shift_two,
    )
    return (grad_first, grad_attended, tail_grads)


def head_backward(inputs, grad_first, grad_query, grad_key, grad_value, qkv_t):
    grad_proj_b = jnp.concatenate([grad_query, grad_key, grad_value], axis=1).astype(jnp.bfloat16)
    grad_qkv_t = mat_tn(grad_proj_b, inputs)
    grad_inputs = grad_first + jnp.dot(grad_proj_b, qkv_t, preferred_element_type=jnp.float32)
    return (grad_inputs, grad_qkv_t, jnp.sum(grad_query, axis=0), jnp.sum(grad_value, axis=0))


def pack_grads(grad_qkv_t, grad_query_b, grad_value_b, tail_grads):
    width = grad_qkv_t.shape[1]
    matrix = jnp.concatenate([grad_qkv_t, tail_grads[0], tail_grads[4], tail_grads[6]], axis=0)
    small = jnp.stack(
        [
            grad_query_b,
            grad_value_b,
            tail_grads[1],
            tail_grads[2],
            tail_grads[3],
            tail_grads[7],
            tail_grads[8],
            tail_grads[9],
        ]
    )
    vectors = jnp.concatenate([small, tail_grads[5].reshape(-1, width)], axis=0)
    return (matrix, vectors)


def adam_update(weights, grads, first, second):
    first_new = beta_one * first + (1.0 - beta_one) * grads
    second_new = beta_two * second + (1.0 - beta_two) * grads * grads
    first_hat = first_new / (1.0 - beta_one**adam_step)
    second_hat = second_new / (1.0 - beta_two**adam_step)
    weights_new = weights - learn_rate * (
        first_hat / (jnp.sqrt(second_hat) + adam_eps) + decay_rate * weights
    )
    return (weights_new, first_new, second_new)


def split_heads(matrix):
    return matrix.reshape(matrix.shape[0], HEADS, matrix.shape[1] // HEADS)


def local(
    tokens,
    cotangent,
    weight_rows,
    first_rows,
    second_rows,
    vector_rows,
    vector_first,
    vector_second,
):
    row_count = tokens.shape[1]
    inputs = tokens.reshape(row_count, D)
    cotan = cotangent.reshape(row_count, D).astype(jnp.float32)
    head_width = D // HEADS
    score_scale = 1.0 / math.sqrt(head_width)
    vectors_b = vector_rows.astype(jnp.bfloat16)
    gathered = lax.all_gather(weight_rows.astype(jnp.bfloat16), "fsdp", axis=0, tiled=True)
    params = unpack(gathered, vectors_b)
    query_rows, key_rows, value_rows = project(inputs, params)
    query_heads = split_heads(query_rows)
    start_state = (
        jnp.full((HEADS, row_count), -jnp.inf, jnp.float32),
        jnp.zeros((HEADS, row_count), jnp.float32),
        jnp.zeros((HEADS, row_count, head_width), jnp.float32),
    )
    key_piece = lax.all_gather(key_rows, "ctx", axis=0, tiled=True)
    value_piece = lax.all_gather(value_rows, "ctx", axis=0, tiled=True)
    amount = key_piece.shape[0]
    block_rows = math.gcd(amount, 512)

    def one_block(position, running):
        row_top, row_total, weighted = running
        key_block = split_heads(
            lax.dynamic_slice_in_dim(key_piece, position * block_rows, block_rows, 0)
        )
        value_block = split_heads(
            lax.dynamic_slice_in_dim(value_piece, position * block_rows, block_rows, 0)
        ).astype(jnp.float32)
        scores = (
            jnp.einsum("qhd,khd->hqk", query_heads, key_block, preferred_element_type=jnp.float32)
            * score_scale
        )
        new_top = jnp.maximum(row_top, jnp.max(scores, axis=-1))
        rescale = jnp.exp(row_top - new_top)
        weights = jnp.exp(scores - new_top[:, :, None])
        row_total = row_total * rescale + jnp.sum(weights, axis=-1)
        weighted = weighted * rescale[:, :, None] + jnp.einsum(
            "hqk,khd->hqd", weights, value_block, precision=lax.Precision.HIGHEST
        )
        return (new_top, row_total, weighted)

    row_top, row_total, weighted = lax.fori_loop(0, amount // block_rows, one_block, start_state)
    attended = (
        (weighted / row_total[:, :, None])
        .transpose(1, 0, 2)
        .reshape(row_count, D)
        .astype(jnp.bfloat16)
    )
    log_totals = row_top + jnp.log(row_total)
    output, saved = tail_forward(inputs, attended, params)
    grad_first, grad_attended, tail_grads = tail_backward(cotan, attended, saved, params)
    grad_heads = split_heads(grad_attended)
    delta = jnp.sum(
        grad_heads.astype(jnp.float32) * split_heads(attended).astype(jnp.float32), axis=-1
    ).T
    seq_length = row_count * lax.axis_size("ctx")
    back_state = (
        jnp.zeros((row_count, HEADS, head_width), jnp.float32),
        jnp.zeros((seq_length, D), jnp.float32),
        jnp.zeros((seq_length, D), jnp.float32),
    )
    attend_key_piece = lax.all_gather(key_rows, "ctx", axis=0, tiled=True)
    attend_value_piece = lax.all_gather(value_rows, "ctx", axis=0, tiled=True)
    amount = attend_key_piece.shape[0]
    attend_block_rows = math.gcd(amount, 512)

    def one_block(position, running):
        grad_query, grad_key, grad_value = running
        offset = position * attend_block_rows
        key_block = split_heads(
            lax.dynamic_slice_in_dim(attend_key_piece, offset, attend_block_rows, 0)
        )
        value_block = split_heads(
            lax.dynamic_slice_in_dim(attend_value_piece, offset, attend_block_rows, 0)
        )
        scores = (
            jnp.einsum("qhd,khd->hqk", query_heads, key_block, preferred_element_type=jnp.float32)
            * score_scale
        )
        probs = jnp.exp(scores - log_totals[:, :, None])
        grad_probs = jnp.einsum(
            "qhd,khd->hqk", grad_heads, value_block, preferred_element_type=jnp.float32
        )
        grad_scores = (probs * (grad_probs - delta[:, :, None])).astype(jnp.bfloat16)
        grad_query = (
            grad_query
            + jnp.einsum("hqk,khd->qhd", grad_scores, key_block, preferred_element_type=jnp.float32)
            * score_scale
        )
        key_term = (
            jnp.einsum("hqk,qhd->khd", grad_scores, query_heads, preferred_element_type=jnp.float32)
            * score_scale
        )
        value_term = jnp.einsum(
            "hqk,qhd->khd",
            probs.astype(jnp.bfloat16),
            grad_heads,
            preferred_element_type=jnp.float32,
        )
        grad_key = lax.dynamic_update_slice_in_dim(
            grad_key, key_term.reshape(attend_block_rows, D), offset, 0
        )
        grad_value = lax.dynamic_update_slice_in_dim(
            grad_value, value_term.reshape(attend_block_rows, D), offset, 0
        )
        return (grad_query, grad_key, grad_value)

    grad_query, grad_key_all, grad_value_all = lax.fori_loop(
        0, amount // attend_block_rows, one_block, back_state
    )
    grad_key, grad_value = (
        lax.psum_scatter(
            grad_key_all.astype(jnp.bfloat16), "ctx", scatter_dimension=0, tiled=True
        ).astype(jnp.float32),
        lax.psum_scatter(
            grad_value_all.astype(jnp.bfloat16), "ctx", scatter_dimension=0, tiled=True
        ).astype(jnp.float32),
    )
    grad_query = grad_query.reshape(row_count, D)
    grad_inputs, grad_qkv_t, grad_query_b, grad_value_b = head_backward(
        inputs, grad_first, grad_query, grad_key, grad_value, params[0]
    )
    matrix, vectors = pack_grads(grad_qkv_t, grad_query_b, grad_value_b, tail_grads)
    vector_total = lax.psum(vectors, ("ctx", "fsdp"))
    new_vectors, new_vfirst, new_vsecond = adam_update(
        vector_rows, vector_total, vector_first, vector_second
    )
    grads = lax.psum_scatter(matrix.astype(jnp.bfloat16), "fsdp", scatter_dimension=0, tiled=True)
    grad_out = lax.psum(grads, "ctx").astype(jnp.float32)
    weights_out, first_out, second_out = adam_update(weight_rows, grad_out, first_rows, second_rows)
    return (
        output.reshape(1, row_count, D),
        grad_inputs.reshape(1, row_count, D),
        grad_out,
        weights_out,
        first_out,
        second_out,
        vector_total,
        new_vectors,
        new_vfirst,
        new_vsecond,
    )


def solution(mesh):
    return jax.shard_map(
        local,
        mesh=mesh,
        in_specs=(
            P("fsdp", "ctx", None),
            P("fsdp", "ctx", None),
            P("fsdp", None),
            P("fsdp", None),
            P("fsdp", None),
            P(),
            P(),
            P(),
        ),
        out_specs=(
            P("fsdp", "ctx", None),
            P("fsdp", "ctx", None),
            P("fsdp", None),
            P("fsdp", None),
            P("fsdp", None),
            P("fsdp", None),
            P(),
            P(),
            P(),
            P(),
        ),
        check_vma=False,
    )
```

profile of v0, /device:TPU:0, one launch (start us, length us, event | category | flops | bytes accessed | tf_op | source)
XLA Modules:
  0.0 671.2 jit_solution(5482531895368750081)
XLA Ops:
  7.2 5.0 convert_element_type.122
  12.3 128.0 %all-gather.4.cloned.1.call-done = bf16[12288,1024]{1,0:T(8,128)(2,1)} async-done(((bf16[1536,1024]{1,0:T(8,128)(2,1)}), bf16[12288,1024]{1,0:T(8,128)(2,1)}) %all-gather.4.cloned.1.call-update) | async-done | bytes 25165840 | tf_op jit(solution)/shard_map/all_gather | solution.py:196
  140.3 5.0 fusion.11
  145.2 0.7 slice.133
  146.1 0.8 fusion.89
  147.0 0.2 copy.29
  147.2 26.9 %all-gather.6.cloned.1.call-done = bf16[512,1024]{1,0:T(8,128)(2,1)} async-done(((bf16[128,1024]{1,0:T(8,128)(2,1)}), bf16[512,1024]{1,0:T(8,128)(2,1)}) %all-gather.6.cloned.1.call-update) | async-done | bytes 1048592 | tf_op jit(solution)/shard_map/all_gather | solution.py:205
  174.1 1.5 copy.30
  175.6 0.8 multiply_reduce_fusion
  176.5 1.2 fusion.19
  177.7 0.8 copy-done
  178.5 25.2 %all-gather.8.cloned.1.call-done = bf16[512,1024]{1,0:T(8,128)(2,1)} async-done(((bf16[128,1024]{1,0:T(8,128)(2,1)}), bf16[512,1024]{1,0:T(8,128)(2,1)}) %all-gather.8.cloned.1.call-update) | async-done | bytes 1048592 | tf_op jit(solution)/shard_map/all_gather | solution.py:206
  203.7 1.5 copy.31
  205.2 5.7 fusion.78
  210.9 2.6 fusion.114
  213.5 0.2 multiply_reduce_fusion.5
  213.8 9.7 %fusion.25 = (bf16[128,4096]{1,0:T(8,128)(2,1)S(1)}, f32[128,4096]{1,0:T(8,128)S(1)}) fusion(f32[4096]{0:T(1024)S(1)} %bitcast.132, bf16[12288,1024]{1,0:T(8,128)(2,1)} %all-gather.4.cloned.1.call-done, f32[128,1024]{1,0:T(8,128)S(1)} %get-tuple-element.103, f32[1024]{0:T(1024)S(1)} %bitcast.121, f32[1024]{0:T(1024)S(1)} %bitcast.113, ...), kind=kOutput, calls=%fused_computation.34 | convolution fusion | flops 1109000192 | bytes 12084224 | tf_op jit(solution)/shard_map/dot_general | solution.py:19
  223.4 5.3 fusion.115
  228.7 0.2 multiply_reduce_fusion.4
  229.0 0.3 fusion.87
  229.3 1.0 fusion.109
  230.2 6.7 fusion.116
  236.9 5.3 multiply_reduce_fusion.1
  242.2 0.2 fusion.111
  242.5 0.8 copy-done.14
  243.2 2.0 fusion.74
  245.5 3.2 fusion.47
  248.7 1.3 copy.35
  250.2 3.9 multiply_convert_fusion
  254.1 1.4 multiply_convert_fusion.1
  255.5 2.3 copy.33
  257.8 0.2 reduce-scatter.8.cloned.1.call-start
  258.1 3.1 convolution_convert_fusion.3
  261.2 1.5 fusion.113
  262.7 5.6 convolution_convert_fusion
  268.3 5.6 convolution_convert_fusion.1
  273.9 2.9 reduce-scatter.12.cloned.1.call-done
  276.8 1.1 copy.36
  278.0 27.4 %reduce-scatter.10.cloned.1.call-done = bf16[128,1024]{1,0:T(8,128)(2,1)} async-done(((bf16[512,1024]{1,0:T(8,128)(2,1)}), bf16[128,1024]{1,0:T(8,128)(2,1)}) %reduce-scatter.10.cloned.1.call-update) | async-done | bytes 262160
  305.4 1.8 copy.34
  307.2 2.9 convolution_convert_fusion.2
  310.1 59.3 %pad_maximum_fusion = bf16[12288,1024]{1,0:T(8,128)(2,1)} fusion(bf16[4096,1024]{1,0:T(8,128)(2,1)} %convolution_convert_fusion, bf16[4096,1024]{1,0:T(8,128)(2,1)} %convolution_convert_fusion.1, bf16[1024,1024]{1,0:T(8,128)(2,1)} %convolution_convert_fusion.3, bf16[3072,1024]{1,0:T(8,128)(2,1)S(1)} %convolution_convert_fusion.2), kind=kLoop, calls=%fused_computation | loop fusion | flops 100663296 | bytes 50331648 | tf_op jit(solution)/shard_map/concatenate | solution.py:148
  369.5 154.8 %reduce-scatter.8.cloned.1.call-done = bf16[1536,1024]{1,0:T(8,128)(2,1)} async-done(((bf16[12288,1024]{1,0:T(8,128)(2,1)}), bf16[1536,1024]{1,0:T(8,128)(2,1)}) %reduce-scatter.8.cloned.1.call-update) | async-done | bytes 3145744 | tf_op jit(solution)/shard_map/reduce_scatter | solution.py:317
  524.8 43.9 %psum.15 = f32[12,1024]{1,0:T(8,128)S(1)} all-reduce(f32[12,1024]{1,0:T(8,128)S(1)} %concatenate.13), channel_id=1, replica_groups=mesh['ctx'=4,'fsdp'=8] {'ctx','fsdp'}, use_global_device_ids=true, to_apply=%region_24.0 | all-reduce | flops 12288 | bytes 98304 | tf_op jit(solution)/shard_map/psum | solution.py:313
  568.7 0.7 multiply_subtract_fusion.1
  569.4 4.6 fusion.71
  574.0 74.7 %all-reduce.2.cloned.1.call-done = bf16[1536,1024]{1,0:T(8,128)(2,1)} async-done(((bf16[1536,1024]{1,0:T(8,128)(2,1)}), bf16[1536,1024]{1,0:T(8,128)(2,1)}) %all-reduce.2.cloned.1.call-update) | async-done | bytes 3145744 | tf_op jit(solution)/shard_map/psum | solution.py:318
  648.8 15.3 %multiply_subtract_fusion = (f32[1536,1024]{1,0:T(8,128)}, f32[1536,1024]{1,0:T(8,128)}, f32[1536,1024]{1,0:T(8,128)}, f32[1536,1024]{1,0:T(8,128)}) fusion(f32[1536,1024]{1,0:T(8,128)} %param.10, f32[1536,1024]{1,0:T(8,128)} %param.11, f32[1536,1024]{1,0:T(8,128)} %param.12, bf16[1536,1024]{1,0:T(8,128)(2,1)} %all-reduce.2.cloned.1.call-done), kind=kLoop, calls=%fused_computation.13 | loop fusion | flops 25165824 | bytes 47185920 | tf_op jit(solution)/shard_map/sub | solution.py:170
  (81 shorter events, 1.2 us)
Async XLA Ops:
  7.2 133.1 %all-gather.4.cloned.1.call-start = ((), (), s32[]{:S(2)}) async-start(), calls=%async_computation.3 | async-start | bytes 28311552 | tf_op jit(solution)/shard_map/all_gather | solution.py:196
  12.2 128.1 %copy-start.20 = (bf16[1,128,1024]{2,1,0:T(8,128)(2,1)S(1)}, bf16[1,128,1024]{2,1,0:T(8,128)(2,1)}, u32[]{:S(2)}) copy-start(bf16[1,128,1024]{2,1,0:T(8,128)(2,1)} %param.8) | copy-start | bytes 786436
  12.2 133.9 %copy-start.21 = (f32[12,1024]{1,0:T(8,128)S(1)}, f32[12,1024]{1,0:T(8,128)}, u32[]{:S(2)}) copy-start(f32[12,1024]{1,0:T(8,128)} %param.13) | copy-start | bytes 147460
  12.2 161.9 %all-gather.6.cloned.1.call-start = ((), (), s32[]{:S(2)}) async-start(), calls=%async_computation.4 | async-start | bytes 1310720 | tf_op jit(solution)/shard_map/all_gather | solution.py:205
  146.0 57.7 %all-gather.8.cloned.1.call-start = ((), (), s32[]{:S(2)}) async-start(), calls=%async_computation.5 | async-start | bytes 1310720 | tf_op jit(solution)/shard_map/all_gather | solution.py:206
  147.0 129.9 %reduce-scatter.12.cloned.1.call-start = ((), (), s32[]{:S(2)}) async-start(), calls=%async_computation.9 | async-start | bytes 1310720
  147.2 29.3 %copy-start.10 = (bf16[128,1024]{0,1:T(8,128)(2,1)}, bf16[128,1024]{0,1:T(8,128)(2,1)S(1)}, u32[]{:S(2)}) copy-start(bf16[128,1024]{0,1:T(8,128)(2,1)S(1)} %copy.29) | copy-start | bytes 786436
  176.5 2.0 copy-start
  205.2 5.7 copy-start.3
  210.9 39.2 %copy-start.18 = (bf16[128,16,64]{0,2,1:T(8,128)(2,1)}, bf16[128,16,64]{0,2,1:T(8,128)(2,1)S(1)}, u32[]{:S(2)}) copy-start(bf16[128,16,64]{0,2,1:T(8,128)(2,1)S(1)} %fusion.78) | copy-start | bytes 786436
  213.5 28.7 %copy-start.1 = (f32[128,1024]{1,0:T(8,128)}, f32[128,1024]{1,0:T(8,128)S(1)}, u32[]{:S(2)}) copy-start(f32[128,1024]{1,0:T(8,128)S(1)} %get-tuple-element.103) | copy-start | bytes 1572868
  223.4 5.3 copy-start.4
  223.4 5.5 copy-start.8
  230.2 6.7 copy-start.12
  236.9 5.3 copy-start.6
  242.4 0.8 copy-start.14
  250.0 55.4 %reduce-scatter.10.cloned.1.call-start = ((), (), s32[]{:S(2)}) async-start(), calls=%async_computation.8 | async-start | bytes 1310720
  250.2 3.9 copy-start.11
  255.5 2.6 copy-start.19
  257.8 266.5 %reduce-scatter.8.cloned.1.call-start = ((), (), s32[]{:S(2)}) async-start(), calls=%async_computation.6 | async-start | bytes 28311552 | tf_op jit(solution)/shard_map/reduce_scatter | solution.py:317
  261.2 1.5 copy-start.5
  261.2 1.5 copy-start.13
  262.7 5.6 copy-start.2
  262.7 5.6 copy-start.7
  369.4 155.0 %copy-start.9 = (bf16[1,128,1024]{2,1,0:T(8,128)(2,1)S(1)}, bf16[1,128,1024]{2,1,0:T(8,128)(2,1)}, u32[]{:S(2)}) copy-start(bf16[1,128,1024]{2,1,0:T(8,128)(2,1)} %param.9) | copy-start | bytes 786436
  369.4 199.3 %copy-start.23 = (f32[12,1024]{1,0:T(8,128)S(1)}, f32[12,1024]{1,0:T(8,128)}, u32[]{:S(2)}) copy-start(f32[12,1024]{1,0:T(8,128)} %param.14) | copy-start | bytes 147460
  369.4 199.3 %copy-start.24 = (f32[12,1024]{1,0:T(8,128)S(1)}, f32[12,1024]{1,0:T(8,128)}, u32[]{:S(2)}) copy-start(f32[12,1024]{1,0:T(8,128)} %param.15) | copy-start | bytes 147460
  369.4 279.3 %all-reduce.2.cloned.1.call-start = ((), (), s32[]{:S(2)}) async-start(), calls=%async_computation.7 | async-start | bytes 6291456 | tf_op jit(solution)/shard_map/psum | solution.py:318
  524.3 45.1 %copy-start.15 = (f32[128,1024]{1,0:T(8,128)S(1)}, f32[128,1024]{1,0:T(8,128)}, u32[]{:S(2)}) copy-start(f32[128,1024]{1,0:T(8,128)} %copy-done.14) | copy-start | bytes 1572868
  524.3 45.1 %copy-start.16 = (bf16[128,1024]{0,1:T(8,128)(2,1)S(1)}, bf16[128,1024]{0,1:T(8,128)(2,1)}, u32[]{:S(2)}) copy-start(bf16[128,1024]{0,1:T(8,128)(2,1)} %copy.34) | copy-start | bytes 786436
  524.3 45.1 %copy-start.17 = (bf16[128,16,64]{0,2,1:T(8,128)(2,1)S(1)}, bf16[128,16,64]{0,2,1:T(8,128)(2,1)}, u32[]{:S(2)}) copy-start(bf16[128,16,64]{0,2,1:T(8,128)(2,1)} %get-tuple-element.89) | copy-start | bytes 786436
  568.7 5.3 copy-start.22
Sparse Core Ops, SparseCore 0:
  12.3 127.9 all-gather.3
  146.1 27.9 all-gather.5
  176.3 27.3 all-gather.7
  250.1 26.6 reduce-scatter.11
  279.6 25.7 reduce-scatter.9
  369.5 154.7 reduce-scatter.7
  526.7 122.0 all-reduce.1
where the time goes:
time: 679 us; the launch traced here: 671 us
  waiting for transfers between devices  440 us (65%)
  other arithmetic  84.5 us (12%)
  matrix products  74.8 us (11%)
  blocking collectives  43.9 us (6%)
  between operations  14.8 us (2%)
  local copies, waits for them, and re-layouts  12.4 us (2%)
    reduce_scatter x1, waiting for transfers between devices, local(): lax.psum_scatter(matrix.astype(jnp.bfloat16), 'fsdp', scatter_dimension=0...  155 us
    all_gather x1, waiting for transfers between devices, local(): lax.all_gather(weight_rows.astype(jnp.bfloat16), 'fsdp', axis=0, tiled=True)  128 us
    psum x1, waiting for transfers between devices, local(): grad_out = lax.psum(grads, 'ctx').astype(jnp.float32)  74.7 us
    concatenate x1, other arithmetic, pack_grads(): jnp.concatenate([grad_qkv_t, tail_grads[0], tail_grads[4], tail_grads[6]]...  59.3 us
    psum x1, blocking collectives, local(): vector_total = lax.psum(vectors, ('ctx', 'fsdp'))  43.9 us
    unnamed x9, waiting for transfers between devices  30.5 us
    all_gather x1, waiting for transfers between devices, local(): key_piece = lax.all_gather(key_rows, 'ctx', axis=0, tiled=True)  26.9 us
    all_gather x1, waiting for transfers between devices, local(): value_piece = lax.all_gather(value_rows, 'ctx', axis=0, tiled=True)  25.2 us
  transfers between devices with their start and end apart: 7, of which 7 were waited for; matrix products, arithmetic and copies ran while one was open for 5% of the time, Pallas kernels for 0%

commit v1 on v0

--- a/solution.py
+++ b/solution.py
@@ -13,6 +13,28 @@
 adam_eps = 1e-08
 norm_eps = 1e-05
 adam_step = 2
+
+
+def laid_out(parts, dim):
+    parts = jnp.moveaxis(parts, 0, dim)
+    shape = parts.shape
+    return parts.reshape(*shape[:dim], shape[dim] * shape[dim + 1], *shape[dim + 2 :])
+
+
+def doubled(array, axis):
+    size = lax.axis_size(axis)
+    blocks = array[None]
+    for level in range(size.bit_length() - 1):
+        stride = 1 << level
+        partner_block = lax.ppermute(blocks, axis, [(i, i ^ stride) for i in range(size)])
+        both = jnp.stack([blocks, partner_block])
+        upper = lax.axis_index(axis) >> level & 1
+        blocks = jnp.where(upper == 0, both, both[::-1]).reshape(-1, *array.shape)
+    return blocks
+
+
+def doubled_up(x, axis, dim):
+    return laid_out(doubled(x, axis), dim)
 
 
 def mat_nt(left, right):
@@ -193,7 +215,7 @@
     head_width = D // HEADS
     score_scale = 1.0 / math.sqrt(head_width)
     vectors_b = vector_rows.astype(jnp.bfloat16)
-    gathered = lax.all_gather(weight_rows.astype(jnp.bfloat16), "fsdp", axis=0, tiled=True)
+    gathered = doubled_up(weight_rows.astype(jnp.bfloat16), "fsdp", 0)
     params = unpack(gathered, vectors_b)
     query_rows, key_rows, value_rows = project(inputs, params)
     query_heads = split_heads(query_rows)

time: 679 us -> 1020 us (1.50)
  waiting for transfers between devices: 440 us -> 723 us
  other arithmetic: 84.5 us -> 140 us
    ppermute x0 -> x3, waiting for transfers between devices: none -> 412 us  [doubled(): lax.ppermute(blocks, axis, [(i, i ^ stride) for i in range(size)])]
    all_gather x1 -> x0, waiting for transfers between devices: 128 us -> none  [local(): lax.all_gather(weight_rows.astype(jnp.bfloat16), 'fsdp', axis=0, tiled=True)]
    another operation x0 -> x5, other arithmetic: none -> 35 us  [doubled(): both = jnp.stack([blocks, partner_block])]
    select_n x0 -> x2, other arithmetic: none -> 23.2 us  [doubled(): blocks = jnp.where(upper == 0, both, both[::-1]).reshape(-1, *array.shape)]
    unnamed x9 -> x8, waiting for transfers between devices: 30.5 us -> 28 us
  transfers between devices with their start and end apart: 7 -> 9, of which waited for: 7 -> 9; matrix products, arithmetic and copies ran while one was open for 5% -> 4% of each run, Pallas kernels for 0% -> 0%
where the time goes in v1:
time: 1020 us; the launch traced here: 1010 us
  waiting for transfers between devices  723 us (71%)
  other arithmetic  140 us (14%)
  matrix products  71.1 us (7%)
  blocking collectives  43.6 us (4%)
  between operations  15.2 us (1%)
  local copies, waits for them, and re-layouts  13.8 us (1%)
    ppermute x3, waiting for transfers between devices, doubled(): lax.ppermute(blocks, axis, [(i, i ^ stride) for i in range(size)])  412 us
    reduce_scatter x1, waiting for transfers between devices, local(): lax.psum_scatter(matrix.astype(jnp.bfloat16), 'fsdp', scatter_dimension=0...  155 us
    psum x1, waiting for transfers between devices, local(): grad_out = lax.psum(grads, 'ctx').astype(jnp.float32)  74.7 us
    concatenate x1, other arithmetic, pack_grads(): jnp.concatenate([grad_qkv_t, tail_grads[0], tail_grads[4], tail_grads[6]]...  59.3 us
    psum x1, blocking collectives, local(): vector_total = lax.psum(vectors, ('ctx', 'fsdp'))  43.6 us
    another operation x5, other arithmetic, doubled(): both = jnp.stack([blocks, partner_block])  35 us
    all_gather x1, waiting for transfers between devices, local(): key_piece = lax.all_gather(key_rows, 'ctx', axis=0, tiled=True)  28.4 us
    unnamed x8, waiting for transfers between devices  28 us
  transfers between devices with their start and end apart: 9, of which 9 were waited for; matrix products, arithmetic and copies ran while one was open for 4% of the time, Pallas kernels for 0%

profile of v1, /device:TPU:0, one launch (start us, length us, event | category | flops | bytes accessed | tf_op | source)
XLA Modules:
  0.0 1012.7 jit_solution(9006029182413581609)
XLA Ops:
  7.2 6.4 convert_bitcast_fusion.1
  14.1 5.5 collective-permute-done
  19.6 1.7 copy-done.1
  21.3 3.4 pad_maximum_fusion.3
  24.7 7.3 fusion.20
  31.9 2.8 collective-permute-start.1
  34.8 136.1 %collective-permute-done.1 = bf16[2,1536,1024]{2,1,0:T(8,128)(2,1)} collective-permute-done((bf16[2,1536,1024]{2,1,0:T(8,128)(2,1)}, bf16[2,1536,1024]{2,1,0:T(8,128)(2,1)}, u32[]{:S(2)}, u32[]{:S(2)}) %collective-permute-start.1) | collective-permute-done | bytes 6291488 | tf_op jit(solution)/shard_map/ppermute | solution.py:29
  170.9 6.1 pad_maximum_fusion.2
  177.0 8.1 reverse_select_fusion.1
  185.1 1.8 collective-permute-start.2
  186.9 270.3 %collective-permute-done.2 = bf16[4,1536,1024]{2,1,0:T(8,128)(2,1)} collective-permute-done((bf16[4,1536,1024]{2,1,0:T(8,128)(2,1)}, bf16[4,1536,1024]{2,1,0:T(8,128)(2,1)}, u32[]{:S(2)}, u32[]{:S(2)}) %collective-permute-start.2) | collective-permute-done | bytes 12582944 | tf_op jit(solution)/shard_map/ppermute | solution.py:29
  457.2 11.8 %pad_maximum_fusion = bf16[2,4,1536,1024]{3,2,1,0:T(8,128)(2,1)S(1)} fusion(bf16[1,4,1536,1024]{3,2,1,0:T(8,128)(2,1)} %bitcast.9, bf16[1,4,1536,1024]{3,2,1,0:T(8,128)(2,1)} %bitcast.7), kind=kLoop, calls=%fused_computation.1 | loop fusion | flops 12582912 | bytes 50331648 | tf_op jit(solution)/shard_map/stack | solution.py:30
  469.0 15.2 %reverse_select_fusion = bf16[2,4,1536,1024]{3,2,1,0:T(8,128)(2,1)} fusion(bf16[2,4,1536,1024]{3,2,1,0:T(8,128)(2,1)S(1)} %pad_maximum_fusion, pred[]{:T(512)S(6)} %eq.9), kind=kLoop, calls=%fused_computation | loop fusion | flops 12582912 | bytes 50331648 | tf_op jit(solution)/shard_map/jit(_where)/select_n | solution.py:32
  484.2 4.6 fusion.21
  490.3 1.0 fusion.94
  492.5 28.4 %all-gather.3.cloned.1.call-done = bf16[512,1024]{0,1:T(8,128)(2,1)} async-done(((bf16[128,1024]{0,1:T(8,128)(2,1)}), bf16[512,1024]{0,1:T(8,128)(2,1)}) %all-gather.3.cloned.1.call-update) | async-done | bytes 1048592 | tf_op jit(solution)/shard_map/all_gather | solution.py:227
  520.9 2.1 multiply_reduce_fusion
  523.0 2.0 copy-done
  525.0 1.2 fusion.24
  526.2 25.0 %all-gather.5.cloned.1.call-done = bf16[512,1024]{0,1:T(8,128)(2,1)} async-done(((bf16[128,1024]{0,1:T(8,128)(2,1)}), bf16[512,1024]{0,1:T(8,128)(2,1)}) %all-gather.5.cloned.1.call-update) | async-done | bytes 1048592 | tf_op jit(solution)/shard_map/all_gather | solution.py:228
  551.3 5.6 fusion.83
  557.0 2.7 fusion.119
  559.9 10.8 %fusion.30 = (bf16[128,4096]{1,0:T(8,128)(2,1)S(1)}, f32[128,4096]{1,0:T(8,128)}) fusion(f32[4096]{0:T(1024)S(1)} %bitcast.159, bf16[12288,1024]{1,0:T(8,128)(2,1)} %bitcast.117, f32[128,1024]{1,0:T(8,128)S(1)} %get-tuple-element.107, f32[1024]{0:T(1024)S(1)} %bitcast.148, f32[1024]{0:T(1024)S(1)} %bitcast.140, f32[128]{0:T(128)S(1)} %add_rsqrt_fusion.1, ...), kind=kOutput, calls=%fused_computation.43 | convolution fusion | flops 1109000192 | bytes 12084224 | tf_op jit(solution)/shard_map/dot_general | solution.py:41
  570.9 1.4 fusion.120
  573.4 1.7 fusion.114
  575.1 6.0 fusion.121
  581.1 3.5 multiply_reduce_fusion.1
  585.6 1.2 fusion.79
  586.8 1.1 copy.19
  587.9 3.2 fusion.52
  591.2 1.3 copy.22
  592.7 3.8 multiply_convert_fusion
  596.5 1.4 multiply_convert_fusion.1
  597.9 2.3 copy.20
  600.5 3.2 convolution_convert_fusion.3
  603.7 2.8 fusion.118
  606.5 5.6 convolution_convert_fusion
  612.1 5.7 convolution_convert_fusion.1
  618.2 1.1 copy.23
  619.4 27.4 %reduce-scatter.10.cloned.1.call-done = bf16[128,1024]{1,0:T(8,128)(2,1)} async-done(((bf16[512,1024]{1,0:T(8,128)(2,1)}), bf16[128,1024]{1,0:T(8,128)(2,1)}) %reduce-scatter.10.cloned.1.call-update) | async-done | bytes 262160
  646.8 1.8 copy.21
  648.6 2.9 convolution_convert_fusion.2
  651.5 59.3 %pad_maximum_fusion.1 = bf16[12288,1024]{1,0:T(8,128)(2,1)} fusion(bf16[4096,1024]{1,0:T(8,128)(2,1)} %convolution_convert_fusion, bf16[4096,1024]{1,0:T(8,128)(2,1)} %convolution_convert_fusion.1, bf16[1024,1024]{1,0:T(8,128)(2,1)} %convolution_convert_fusion.3, bf16[3072,1024]{1,0:T(8,128)(2,1)S(1)} %convolution_convert_fusion.2), kind=kLoop, calls=%fused_computation.2 | loop fusion | flops 100663296 | bytes 50331648 | tf_op jit(solution)/shard_map/concatenate | solution.py:170
  711.0 154.9 %reduce-scatter.8.cloned.1.call-done = bf16[1536,1024]{1,0:T(8,128)(2,1)} async-done(((bf16[12288,1024]{1,0:T(8,128)(2,1)}), bf16[1536,1024]{1,0:T(8,128)(2,1)}) %reduce-scatter.8.cloned.1.call-update) | async-done | bytes 3145744 | tf_op jit(solution)/shard_map/reduce_scatter | solution.py:339
  866.3 43.6 %psum.15 = f32[12,1024]{1,0:T(8,128)S(1)} all-reduce(f32[12,1024]{1,0:T(8,128)S(1)} %concatenate.13), channel_id=1, replica_groups=mesh['ctx'=4,'fsdp'=8] {'ctx','fsdp'}, use_global_device_ids=true, to_apply=%region_24.25 | all-reduce | flops 12288 | bytes 98304 | tf_op jit(solution)/shard_map/psum | solution.py:335
  910.7 4.6 fusion.76
  915.4 74.7 %all-reduce.2.cloned.1.call-done = bf16[1536,1024]{1,0:T(8,128)(2,1)} async-done(((bf16[1536,1024]{1,0:T(8,128)(2,1)}), bf16[1536,1024]{1,0:T(8,128)(2,1)}) %all-reduce.2.cloned.1.call-update) | async-done | bytes 3145744 | tf_op jit(solution)/shard_map/psum | solution.py:340
  990.1 15.3 %multiply_subtract_fusion = (f32[1536,1024]{1,0:T(8,128)}, f32[1536,1024]{1,0:T(8,128)}, f32[1536,1024]{1,0:T(8,128)}, f32[1536,1024]{1,0:T(8,128)}) fusion(f32[1536,1024]{1,0:T(8,128)} %param.10, f32[1536,1024]{1,0:T(8,128)} %param.11, f32[1536,1024]{1,0:T(8,128)} %param.12, bf16[1536,1024]{1,0:T(8,128)(2,1)} %all-reduce.2.cloned.1.call-done), kind=kLoop, calls=%fused_computation.19 | loop fusion | flops 25165824 | bytes 47185920 | tf_op jit(solution)/shard_map/sub | solution.py:192
  (126 shorter events, 7.6 us)
Async XLA Ops:
  7.2 513.7 %all-gather.3.cloned.1.call-start = ((), (), s32[]{:S(2)}) async-start(), calls=%async_computation.3 | async-start | bytes 1310720 | tf_op jit(solution)/shard_map/all_gather | solution.py:227
  13.6 6.0 collective-permute-start
  31.9 139.0 %collective-permute-start.1 = (bf16[2,1536,1024]{2,1,0:T(8,128)(2,1)}, bf16[2,1536,1024]{2,1,0:T(8,128)(2,1)}, u32[]{:S(2)}, u32[]{:S(2)}) collective-permute-start(bf16[2,1536,1024]{2,1,0:T(8,128)(2,1)} %get-tuple-element.86), channel_id=1, source_target_pairs={{0,2},{1,3},{2,0},{3,1},{4,6},{5,7},{6,4},{7,5},{8,10},{9,11},{10,... | collective-permute-start | bytes 18874376 | tf_op jit(solution)/shard_map/ppermute | solution.py:29
  185.1 272.1 %collective-permute-start.2 = (bf16[4,1536,1024]{2,1,0:T(8,128)(2,1)}, bf16[4,1536,1024]{2,1,0:T(8,128)(2,1)}, u32[]{:S(2)}, u32[]{:S(2)}) collective-permute-start(bf16[4,1536,1024]{2,1,0:T(8,128)(2,1)} %bitcast.8), channel_id=1, source_target_pairs={{0,4},{1,5},{2,6},{3,7},{4,0},{5,1},{6,2},{7,3},{8,12},{9,13},{10,... | collective-permute-start | bytes 37748744 | tf_op jit(solution)/shard_map/ppermute | solution.py:29
  469.0 15.2 %copy-start.16 = (bf16[1,128,1024]{2,1,0:T(8,128)(2,1)S(1)}, bf16[1,128,1024]{2,1,0:T(8,128)(2,1)}, u32[]{:S(2)}) copy-start(bf16[1,128,1024]{2,1,0:T(8,128)(2,1)} %param.8) | copy-start | bytes 786436
  484.2 5.4 copy-start.17
  489.6 61.7 %all-gather.5.cloned.1.call-start = ((), (), s32[]{:S(2)}) async-start(), calls=%async_computation.4 | async-start | bytes 1310720 | tf_op jit(solution)/shard_map/all_gather | solution.py:228
  491.3 34.9 %copy-start.7 = (bf16[128,1024]{0,1:T(8,128)(2,1)}, bf16[128,1024]{0,1:T(8,128)(2,1)S(1)}, u32[]{:S(2)}) copy-start(bf16[128,1024]{0,1:T(8,128)(2,1)S(1)} %get-tuple-element.89) | copy-start | bytes 786436
  491.3 126.9 %reduce-scatter.12.cloned.1.call-start = ((), (), s32[]{:S(2)}) async-start(), calls=%async_computation.8 | async-start | bytes 1310720
  551.3 8.6 copy-start.21
  551.3 8.6 copy-start.27
  556.9 2.9 copy-start.14
  556.9 13.9 %slice-start = ((s8[25165824]{0:T(1024)(128)(4,1)}), s8[4194304]{0:T(1024)(128)(4,1)S(1)}, s32[]{:S(2)}) async-start(s8[25165824]{0:T(1024)(128)(4,1)} %bitcast.119), calls=%async_computation.9 | async-start | bytes 8388608
  559.6 11.2 %copy-start.28 = (f32[128]{0:T(128)}, f32[128]{0:T(128)S(1)}, u32[]{:S(2)}) copy-start(f32[128]{0:T(128)S(1)} %broadcast_multiply_fusion.5) | copy-start | bytes 1540
  559.8 11.0 %copy-start.35 = (f32[128]{0:T(128)}, f32[128]{0:T(128)S(1)}, u32[]{:S(2)}) copy-start(f32[128]{0:T(128)S(1)} %add_rsqrt_fusion.1) | copy-start | bytes 1540
  559.9 10.9 %slice-start.1 = ((s8[25165824]{0:T(1024)(128)(4,1)}), s8[4194304]{0:T(1024)(128)(4,1)S(1)}, s32[]{:S(2)}) async-start(s8[25165824]{0:T(1024)(128)(4,1)} %bitcast.119), calls=%async_computation.10 | async-start | bytes 8388608
  559.9 10.9 %slice-start.2 = ((s8[25165824]{0:T(1024)(128)(4,1)}), s8[4194304]{0:T(1024)(128)(4,1)S(1)}, s32[]{:S(2)}) async-start(s8[25165824]{0:T(1024)(128)(4,1)} %bitcast.119), calls=%async_computation.11 | async-start | bytes 8388608
  559.9 10.9 %slice-start.3 = ((s8[25165824]{0:T(1024)(128)(4,1)}), s8[4194304]{0:T(1024)(128)(4,1)S(1)}, s32[]{:S(2)}) async-start(s8[25165824]{0:T(1024)(128)(4,1)} %bitcast.119), calls=%async_computation.12 | async-start | bytes 8388608
  559.9 10.9 %slice-start.4 = ((s8[25165824]{0:T(1024)(128)(4,1)}), s8[4194304]{0:T(1024)(128)(4,1)S(1)}, s32[]{:S(2)}) async-start(s8[25165824]{0:T(1024)(128)(4,1)} %bitcast.119), calls=%async_computation.13 | async-start | bytes 8388608
  559.9 10.9 %slice-start.5 = ((s8[25165824]{0:T(1024)(128)(4,1)}), s8[4194304]{0:T(1024)(128)(4,1)S(1)}, s32[]{:S(2)}) async-start(s8[25165824]{0:T(1024)(128)(4,1)} %bitcast.119), calls=%async_computation.14 | async-start | bytes 8388608
  559.9 10.9 %copy-start.34 = (f32[1,1024]{1,0:T(1,128)S(1)}, f32[1,1024]{1,0:T(1,128)}, u32[]{:S(2)}) copy-start(f32[1,1024]{1,0:T(1,128)} %get-tuple-element.96) | copy-start | bytes 12292
  570.9 2.5 copy-start.25
  575.1 6.0 copy-start.29
  581.1 3.5 copy-start.30
  581.1 3.5 copy-start.36
  587.9 4.7 copy-start.15
  592.5 4.0 copy-start.8
  592.5 54.3 %reduce-scatter.10.cloned.1.call-start = ((), (), s32[]{:S(2)}) async-start(), calls=%async_computation.7 | async-start | bytes 1310720
  600.2 6.3 copy-start.9
  600.2 265.6 %reduce-scatter.8.cloned.1.call-start = ((), (), s32[]{:S(2)}) async-start(), calls=%async_computation.5 | async-start | bytes 28311552 | tf_op jit(solution)/shard_map/reduce_scatter | solution.py:339
  600.5 6.0 copy-start.3
  606.5 5.6 copy-start.4
  606.5 5.6 copy-start.22
  606.5 5.6 copy-start.31
  606.5 5.6 copy-start.37
  710.8 155.1 %copy-start.6 = (bf16[1,128,1024]{2,1,0:T(8,128)(2,1)S(1)}, bf16[1,128,1024]{2,1,0:T(8,128)(2,1)}, u32[]{:S(2)}) copy-start(bf16[1,128,1024]{2,1,0:T(8,128)(2,1)} %param.9) | copy-start | bytes 786436
  710.8 155.2 %copy-start.26 = (f32[4096]{0:T(1024)S(1)}, f32[4096]{0:T(1024)}, u32[]{:S(2)}) copy-start(f32[4096]{0:T(1024)} %get-tuple-element.114) | copy-start | bytes 49156
  710.8 155.4 %copy-start.23 = (f32[1024]{0:T(1024)S(1)}, f32[1024]{0:T(1024)}, u32[]{:S(2)}) copy-start(f32[1024]{0:T(1024)} %get-tuple-element.58) | copy-start | bytes 12292
  710.8 155.4 %copy-start.24 = (f32[1024]{0:T(1024)S(1)}, f32[1024]{0:T(1024)}, u32[]{:S(2)}) copy-start(f32[1024]{0:T(1024)} %get-tuple-element.77) | copy-start | bytes 12292
  710.8 155.4 %copy-start.32 = (f32[1024]{0:T(1024)S(1)}, f32[1024]{0:T(1024)}, u32[]{:S(2)}) copy-start(f32[1024]{0:T(1024)} %get-tuple-element.56) | copy-start | bytes 12292
  710.9 155.4 %copy-start.33 = (f32[1024]{0:T(1024)S(1)}, f32[1024]{0:T(1024)}, u32[]{:S(2)}) copy-start(f32[1024]{0:T(1024)} %get-tuple-element.61) | copy-start | bytes 12292
  710.9 199.1 %copy-start.19 = (f32[12,1024]{1,0:T(8,128)S(1)}, f32[12,1024]{1,0:T(8,128)}, u32[]{:S(2)}) copy-start(f32[12,1024]{1,0:T(8,128)} %param.14) | copy-start | bytes 147460
  710.9 199.1 %copy-start.20 = (f32[12,1024]{1,0:T(8,128)S(1)}, f32[12,1024]{1,0:T(8,128)}, u32[]{:S(2)}) copy-start(f32[12,1024]{1,0:T(8,128)} %param.15) | copy-start | bytes 147460
  710.9 199.8 %copy-start.11 = (f32[128,1024]{1,0:T(8,128)S(1)}, f32[128,1024]{1,0:T(8,128)}, u32[]{:S(2)}) copy-start(f32[128,1024]{1,0:T(8,128)} %copy-done.10) | copy-start | bytes 1572868
  710.9 199.8 %copy-start.12 = (bf16[128,1024]{0,1:T(8,128)(2,1)S(1)}, bf16[128,1024]{0,1:T(8,128)(2,1)}, u32[]{:S(2)}) copy-start(bf16[128,1024]{0,1:T(8,128)(2,1)} %copy.21) | copy-start | bytes 786436
  710.9 199.8 %copy-start.13 = (bf16[128,16,64]{0,2,1:T(8,128)(2,1)S(1)}, bf16[128,16,64]{0,2,1:T(8,128)(2,1)}, u32[]{:S(2)}) copy-start(bf16[128,16,64]{0,2,1:T(8,128)(2,1)} %get-tuple-element.93) | copy-start | bytes 786436
  710.9 279.1 %all-reduce.2.cloned.1.call-start = ((), (), s32[]{:S(2)}) async-start(), calls=%async_computation.6 | async-start | bytes 6291456 | tf_op jit(solution)/shard_map/psum | solution.py:340
  910.0 5.3 copy-start.18
  (5 other events, 7.8 us)
Sparse Core Ops, SparseCore 0:
  489.7 31.1 all-gather.2
  523.0 28.2 all-gather.4
  592.6 25.5 reduce-scatter.11
  621.0 25.7 reduce-scatter.9
  711.0 154.7 reduce-scatter.7
  868.1 121.9 all-reduce.1
